TPU v7x, 256 devices: a whole 4x4x8 slice. The times are simulated.
256 devices in a mesh: row: 16 (over z, core), col: 16 (over x, y).
Axes of the slice: x: 4, y: 4, z: 8, core: 2. Of those that a mesh axis runs over, the one named last changes fastest.
Arguments:
- tile_values: float32 [12288, 32, 1024], P(('row', 'col')), may hold values from -6 to 6
- tile_count: int32 [256], P(('row', 'col')), may hold values from 1 to 48, as said below
- mode1_column: int32 [12288, 1], P(('row', 'col')), may hold values from 0 to 15; in each aligned block of 48 rows (0 to 47, 48 to 95, ...) at most 4 rows name the same one
- mode1_offset: int32 [12288], P(('row', 'col')), may hold values from 0 to 15
- mode2_row: int32 [12288, 1], P(('row', 'col')), may hold values from 0 to 15; in each aligned block of 48 rows (0 to 47, 48 to 95, ...) at most 4 rows name the same one
- mode2_offset: int32 [12288], P(('row', 'col')), may hold values from 0 to 7
- mode3_offset: int32 [12288], P(('row', 'col')), may hold values from 0 to 15
- mode2_factor: float32 [65536, 256], P(('row', 'col'))
- mode3_factor: float32 [8192, 256], P('col')
Outputs:
- updated: float32 [131072, 256], P(('row', 'col'))
Inputs may be any that keep to these rules, and one draw needn't show every extreme that they name: Device d's live tiles fill its first tile_count[d] slots; other slots are ignored. Some device holds 48 live tiles. `mode1_column`: at most 4 slots of one device name the same value, and some device reaches it. `mode2_row`: at most 4 slots of one device name the same value, and some device reaches it.
All inputs are finite; a program needn't handle non-finite values.
Results may differ from a plain program's by a relative error of at most 0.0003.
Values sent between devices are 32-bit elements; how exact they have to be, the bound alone decides.
No kernel may reach another device: no remote copies, remote signals or barrier semaphores. Data moves between devices by JAX's collectives and lax.ppermute only.
A program may use at most 128 MiB of HBM per device.

v0:
```python
import jax
import jax.numpy as jnp
from jax import lax
from jax.sharding import PartitionSpec as P

IB_DEV = 16
HIGHEST_PRECISION = lax.Precision.HIGHEST


def product_of(left_matrix, right_matrix):
    return lax.dot_general(
        left_matrix,
        right_matrix,
        (((0,), (0,)), ((), ())),
        precision=HIGHEST_PRECISION,
        preferred_element_type=jnp.float32,
    )


def local(
    tile_values,
    tile_count,
    mode1_column,
    mode1_offset,
    mode2_row,
    mode2_offset,
    mode3_offset,
    mode2_factor,
    mode3_factor,
):
    slot_count = tile_values.shape[0]
    tile_edge = tile_values.shape[1]
    rank_width = mode2_factor.shape[1]
    rows_held = mode2_factor.shape[0]
    col_index = lax.axis_index("col")
    live_count = tile_count[0]
    slot_index = jnp.arange(slot_count, dtype=jnp.int32)
    is_live = slot_index < live_count
    tile_lines = jnp.arange(tile_edge, dtype=jnp.int32)
    owner_row = jnp.where(is_live, mode2_row[:, 0], -1)
    owner_col = jnp.where(is_live, mode1_column[:, 0], -1)
    own_second = product_of(mode2_factor, mode2_factor)
    own_third = product_of(mode3_factor, mode3_factor)
    sum_second = lax.psum(own_second, ("row", "col"))
    sum_third = lax.psum(own_third, "col")
    normal_matrix = sum_second * sum_third
    wanted = (owner_row * rows_held + mode2_offset * tile_edge)[:, None] + tile_lines[None, :]
    shard_piece = lax.all_gather(mode2_factor, "row", axis=0, tiled=True)
    piece_length = shard_piece.shape[0]
    inside = (wanted >= 0) & (wanted < piece_length)
    taken = jnp.take(shard_piece, jnp.clip(wanted, 0, piece_length - 1).reshape(-1), axis=0)
    taken = taken.reshape(slot_count, tile_edge, rank_width)
    picked = jnp.where(inside[:, :, None], taken, 0.0)
    third_index = (mode3_offset * tile_edge)[:, None] + tile_lines[None, :]
    mode3_rows = jnp.take(mode3_factor, third_index.reshape(-1), axis=0).reshape(
        slot_count, tile_edge, rank_width
    )
    group_size = min(8, slot_count)
    group_total = (live_count + group_size - 1) // group_size

    def contract(group_at, partials):
        start_slot = jnp.minimum(group_at * group_size, slot_count - group_size).astype(jnp.int32)
        second_part = lax.dynamic_slice_in_dim(picked, start_slot, group_size, 0)
        third_part = lax.dynamic_slice_in_dim(mode3_rows, start_slot, group_size, 0)
        values_part = lax.dynamic_slice_in_dim(tile_values, start_slot, group_size, 0)
        khatri = (second_part[:, :, None, :] * third_part[:, None, :, :]).reshape(
            group_size, tile_edge * tile_edge, rank_width
        )
        product_rows = jnp.einsum("gie,ger->gir", values_part, khatri, precision=HIGHEST_PRECISION)
        return lax.dynamic_update_slice_in_dim(partials, product_rows, start_slot, 0)

    partials = lax.fori_loop(
        0, group_total, contract, jnp.zeros((slot_count, tile_edge, rank_width), jnp.float32)
    )
    sent_targets = jnp.where(is_live, owner_col * IB_DEV + mode1_offset, -1).astype(jnp.float32)
    own_blocks = (col_index * IB_DEV + jnp.arange(IB_DEV, dtype=jnp.int32)).astype(jnp.float32)
    gathered_rows = lax.all_gather(partials, "col", axis=0, tiled=True)
    gathered_targets = lax.all_gather(sent_targets, "col", axis=0, tiled=True)
    selector = (gathered_targets[:, None] == own_blocks[None, :]).astype(jnp.float32)
    mttkrp = jnp.einsum("pb,pir->bir", selector, gathered_rows, precision=HIGHEST_PRECISION)
    cholesky_factor = jnp.linalg.cholesky(normal_matrix)
    mttkrp_rows = mttkrp.reshape(IB_DEV * tile_edge, rank_width)
    return jax.scipy.linalg.cho_solve((cholesky_factor, True), mttkrp_rows.T).T


def solution(mesh):
    placed = (
        P(("row", "col"), None, None),
        P(("row", "col")),
        P(("row", "col"), None),
        P(("row", "col")),
        P(("row", "col"), None),
        P(("row", "col")),
        P(("row", "col")),
        P(("row", "col"), None),
        P("col", None),
    )
    return jax.shard_map(
        local, mesh=mesh, in_specs=placed, out_specs=P(("row", "col"), None), check_vma=False
    )
```

profile of v0, /device:TPU:1, one launch (start us, length us, event | category | flops | bytes accessed | tf_op | source)
XLA Modules:
  0.0 551.6 jit_solution(1135849408825072373)
XLA Ops:
  8.2 2.3 fusion.31
  10.6 1.7 fusion.32
  13.7 3.7 gather_fusion.1
  17.4 1.5 broadcast_select_fusion
  18.8 37.9 %all-gather.3.cloned.1.call-done = f32[4096,256]{1,0:T(8,128)} async-done(((f32[256,256]{1,0:T(8,128)}), f32[4096,256]{1,0:T(8,128)}) %all-gather.3.cloned.1.call-update) | async-done | bytes 4194320 | tf_op jit(solution)/shard_map/all_gather | solution.py:48
  56.7 5.9 %gather_fusion = f32[1536,256]{1,0:T(8,128)S(1)} fusion(f32[4096,256]{1,0:T(8,128)} %all-gather.3.cloned.1.call-done, s32[2048]{0:T(1024)S(1)} %pad_clamp_fusion.1), kind=kCustom, calls=%fused_computation | custom fusion | bytes 3151872 | tf_op jit(solution)/shard_map/jit(_take)/gather | solution.py:51
  62.6 1.5 select_select_fusion
  64.2 53.0 %while.11 = (s32[]{:T(128)}, f32[48,32,256]{2,0,1:T(8,128)S(1)}, s32[]{:T(128)}, f32[48,32,1024]{2,1,0:T(8,128)}, f32[48,32,256]{2,1,0:T(8,128)}, /*index=5*/f32...) while((s32[]{:T(128)}, f32[48,32,256]{2,0,1:T(8,128)S(1)}, ...), condition=%wide.region_7.8_spmd, body=%wide.region_6.7_spmd.sunk | while | flops 807403520 | bytes 20709556 | solution.py:72
  66.5 6.1 %fusion.52 = f32[8,32,256]{2,1,0:T(8,128)S(1)} fusion(f32[8,1024,256]{2,1,0:T(8,128)S(1)} %bitcast.78, f32[48,32,1024]{2,1,0:T(8,128)} %get-tuple-element.177, s32[]{:T(128)S(6)} %select_n.118), kind=kOutput, calls=%fused_computation.3.clone.1 | convolution fusion | flops 805306368 | bytes 9699332 | tf_op jit(solution)/shard_map/while/body/gie,ger->gir/dot_general | solution.py:69
  75.3 6.1 %fusion.52 = f32[8,32,256]{2,1,0:T(8,128)S(1)} fusion(f32[8,1024,256]{2,1,0:T(8,128)S(1)} %bitcast.78, f32[48,32,1024]{2,1,0:T(8,128)} %get-tuple-element.177, s32[]{:T(128)S(6)} %select_n.118), kind=kOutput, calls=%fused_computation.3.clone.1 | convolution fusion | flops 805306368 | bytes 9699332 | tf_op jit(solution)/shard_map/while/body/gie,ger->gir/dot_general | solution.py:69
  84.2 6.1 %fusion.52 = f32[8,32,256]{2,1,0:T(8,128)S(1)} fusion(f32[8,1024,256]{2,1,0:T(8,128)S(1)} %bitcast.78, f32[48,32,1024]{2,1,0:T(8,128)} %get-tuple-element.177, s32[]{:T(128)S(6)} %select_n.118), kind=kOutput, calls=%fused_computation.3.clone.1 | convolution fusion | flops 805306368 | bytes 9699332 | tf_op jit(solution)/shard_map/while/body/gie,ger->gir/dot_general | solution.py:69
  93.0 6.1 %fusion.52 = f32[8,32,256]{2,1,0:T(8,128)S(1)} fusion(f32[8,1024,256]{2,1,0:T(8,128)S(1)} %bitcast.78, f32[48,32,1024]{2,1,0:T(8,128)} %get-tuple-element.177, s32[]{:T(128)S(6)} %select_n.118), kind=kOutput, calls=%fused_computation.3.clone.1 | convolution fusion | flops 805306368 | bytes 9699332 | tf_op jit(solution)/shard_map/while/body/gie,ger->gir/dot_general | solution.py:69
  101.8 6.1 %fusion.52 = f32[8,32,256]{2,1,0:T(8,128)S(1)} fusion(f32[8,1024,256]{2,1,0:T(8,128)S(1)} %bitcast.78, f32[48,32,1024]{2,1,0:T(8,128)} %get-tuple-element.177, s32[]{:T(128)S(6)} %select_n.118), kind=kOutput, calls=%fused_computation.3.clone.1 | convolution fusion | flops 805306368 | bytes 9699332 | tf_op jit(solution)/shard_map/while/body/gie,ger->gir/dot_general | solution.py:69
  110.7 6.1 %fusion.52 = f32[8,32,256]{2,1,0:T(8,128)S(1)} fusion(f32[8,1024,256]{2,1,0:T(8,128)S(1)} %bitcast.78, f32[48,32,1024]{2,1,0:T(8,128)} %get-tuple-element.177, s32[]{:T(128)S(6)} %select_n.118), kind=kOutput, calls=%fused_computation.3.clone.1 | convolution fusion | flops 805306368 | bytes 9699332 | tf_op jit(solution)/shard_map/while/body/gie,ger->gir/dot_general | solution.py:69
  119.8 29.3 %all-reduce.1 = f32[768]{0:T(1024)S(1)} all-reduce(f32[768]{0:T(1024)S(1)} %convert_dynamic-update-slice_fusion), channel_id=1, replica_groups=mesh['row'=16,'col'=16] {'col'}, use_global_device_ids=true, to_apply=%add.1 | all-reduce | flops 768 | bytes 6144
  149.1 120.2 %all-reduce.5.cloned.1.call-done = f32[256,256]{0,1:T(8,128)} async-done(((f32[256,256]{0,1:T(8,128)}), f32[256,256]{0,1:T(8,128)}) %all-reduce.5.cloned.1.call-update) | async-done | bytes 262160 | tf_op jit(solution)/shard_map/psum | solution.py:44
  269.4 95.4 %all-reduce.7.cloned.1.call-done = f32[256,256]{0,1:T(8,128)} async-done(((f32[256,256]{0,1:T(8,128)}), f32[256,256]{0,1:T(8,128)}) %all-reduce.7.cloned.1.call-update) | async-done | bytes 262160 | tf_op jit(solution)/shard_map/psum | solution.py:45
  366.0 11.7 %cholesky.50 = f32[128,128]{1,0:T(8,128)S(1)} custom-call(f32[128,128]{1,0:T(8,128)S(1)} %cholesky.118), custom_call_target="Cholesky" | custom-call | tf_op jit(solution)/shard_map/jit(cholesky)/cholesky | solution.py:81
  377.8 9.8 %custom-call.18 = f32[1,128,128]{1,2,0:T(8,128)S(1)} custom-call(f32[1,128,128]{2,1,0:T(8,128)S(1)} %get-tuple-element.74), custom_call_target="InvertDiagBlocksLowerTriangular" | custom-call | tf_op jit(solution)/shard_map/jit(cholesky)/cholesky | solution.py:81
  388.1 11.7 %cholesky.105 = f32[128,128]{1,0:T(8,128)S(1)} custom-call(f32[128,128]{1,0:T(8,128)S(1)} %convolution_subtract_fusion.2), custom_call_target="Cholesky" | custom-call | tf_op jit(solution)/shard_map/jit(cholesky)/cholesky | solution.py:81
  402.0 4.3 while.12
  406.3 19.7 %custom-call.19 = f32[2,128,128]{1,2,0:T(8,128)S(1)} custom-call(f32[2,128,128]{2,1,0:T(8,128)S(1)} %get-tuple-element.46), custom_call_target="InvertDiagBlocksLowerTriangular" | custom-call | tf_op jit(solution)/shard_map/jit(_cho_solve)/triangular_solve | solution.py:83
  426.0 101.7 %all-gather.5.cloned.1.call-done = f32[768,32,256]{2,0,1:T(8,128)} async-done(((f32[48,32,256]{2,0,1:T(8,128)}), f32[768,32,256]{2,0,1:T(8,128)}) %all-gather.5.cloned.1.call-update) | async-done | bytes 25165840 | tf_op jit(solution)/shard_map/all_gather | solution.py:77
  527.7 12.3 %fusion.14 = f32[16,32,256]{2,0,1:T(8,128)S(1)} fusion(f32[768,32,256]{2,0,1:T(8,128)} %all-gather.5.cloned.1.call-done, f32[768]{0:T(1024)S(1)} %all-reduce.1, f32[16]{0:T(128)S(1)} %add_convert_fusion), kind=kOutput, calls=%fused_computation.39 | convolution fusion | flops 1207971840 | bytes 25693248 | tf_op jit(solution)/shard_map/pb,pir->bir/dot_general | solution.py:80
  (94 shorter events, 30.2 us)
Async XLA Ops:
  7.4 3.2 copy-start
  7.4 5.7 %copy-start.4 = (s32[48,1]{0,1:T(1,128)S(1)}, s32[48,1]{0,1:T(1,128)}, u32[]{:S(2)}) copy-start(s32[48,1]{0,1:T(1,128)} %param.15) | copy-start | bytes 580
  7.4 5.7 %copy-start.5 = (s32[48]{0:T(128)S(1)}, s32[48]{0:T(128)}, u32[]{:S(2)}) copy-start(s32[48]{0:T(128)} %param.16) | copy-start | bytes 580
  7.4 5.9 %copy-start.6 = (s32[48]{0:T(128)S(1)}, s32[48]{0:T(128)}, u32[]{:S(2)}) copy-start(s32[48]{0:T(128)} %param.17) | copy-start | bytes 580
  7.4 49.3 %all-gather.3.cloned.1.call-start = ((), (), s32[]{:S(2)}) async-start(), calls=%async_computation.2 | async-start | bytes 4456448 | tf_op jit(solution)/shard_map/all_gather | solution.py:48
  8.1 261.3 %all-reduce.5.cloned.1.call-start = ((), (), s32[]{:S(2)}) async-start(), calls=%async_computation | async-start | bytes 524288 | tf_op jit(solution)/shard_map/psum | solution.py:44
  10.5 354.3 %all-reduce.7.cloned.1.call-start = ((), (), s32[]{:S(2)}) async-start(), calls=%async_computation.1 | async-start | bytes 524288 | tf_op jit(solution)/shard_map/psum | solution.py:45
  12.3 515.3 %all-gather.5.cloned.1.call-start = ((), (), s32[]{:S(2)}) async-start(), calls=%async_computation.3 | async-start | bytes 26738688 | tf_op jit(solution)/shard_map/all_gather | solution.py:77
  117.2 1.2 copy-start.1
  117.2 1.3 copy-start.7
  117.3 2.4 copy-start.2
  117.3 2.4 copy-start.3
Sparse Core Ops, SparseCore 0:
  10.2 46.4 all-gather.2
Sparse Core Ops, SparseCore 1:
  14.0 255.3 all-reduce.4
  272.4 92.3 all-reduce.6
  367.4 160.2 all-gather.4
where the time goes:
time: 552 us
  waiting for transfers between devices  356 us (64%)
  other arithmetic  65.2 us (12%)
  matrix products  56.1 us (10%)
  blocking collectives  29.3 us (5%)
  local copies, waits for them, and re-layouts  26.3 us (5%)
  between operations  18 us (3%)
    psum x1, waiting for transfers between devices, local(): sum_second = lax.psum(own_second, ('row', 'col'))  120 us
    all_gather x1, waiting for transfers between devices, local(): gathered_rows = lax.all_gather(partials, 'col', axis=0, tiled=True)  102 us
    psum x1, waiting for transfers between devices, local(): sum_third = lax.psum(own_third, 'col')  95.4 us
    all_gather x1, waiting for transfers between devices, local(): shard_piece = lax.all_gather(mode2_factor, 'row', axis=0, tiled=True)  37.9 us
    dot_general x6, matrix products, contract(): jnp.einsum('gie,ger->gir', values_part, khatri, precision=HIGHEST_PRECISION)  36.6 us
    another operation x6, other arithmetic, local(): cholesky_factor = jnp.linalg.cholesky(normal_matrix)  34 us
    unnamed x1, blocking collectives  29.3 us
    another operation x3, other arithmetic, local(): return jax.scipy.linalg.cho_solve((cholesky_factor, True), mttkrp_rows.T).T  19.7 us
  transfers between devices with their start and end apart: 4, of which 4 were waited for; matrix products, arithmetic and copies ran while one was open for 24% of the time, Pallas kernels for 0%

commit v1 on v0

--- a/solution.py
+++ b/solution.py
@@ -74,7 +74,9 @@
     )
     sent_targets = jnp.where(is_live, owner_col * IB_DEV + mode1_offset, -1).astype(jnp.float32)
     own_blocks = (col_index * IB_DEV + jnp.arange(IB_DEV, dtype=jnp.int32)).astype(jnp.float32)
-    gathered_rows = lax.all_gather(partials, "col", axis=0, tiled=True)
+    gathered_rows = jnp.concatenate(
+        lax.all_to_all(jnp.stack([partials] * lax.axis_size("col")), "col", 0, 0), axis=0
+    )
     gathered_targets = lax.all_gather(sent_targets, "col", axis=0, tiled=True)
     selector = (gathered_targets[:, None] == own_blocks[None, :]).astype(jnp.float32)
     mttkrp = jnp.einsum("pb,pir->bir", selector, gathered_rows, precision=HIGHEST_PRECISION)

time: 552 us -> 906 us (1.64)
  blocking collectives: 29.3 us -> 469 us
  waiting for transfers between devices: 356 us -> 247 us
  local copies, waits for them, and re-layouts: 26.3 us -> 46.8 us
    unnamed x1, blocking collectives: 29.3 us -> 469 us
    all_gather x1 -> x0, waiting for transfers between devices: 102 us -> none  [local(): gathered_rows = lax.all_gather(partials, 'col', axis=0, tiled=True)]
    another operation x6 -> x7, local copies, waits for them, and re-layouts: 4.06 us -> 15.5 us  [the longest x1 11.6 us: local(): jnp.stack([partials] * lax.axis_size('col'))]
    psum x1, waiting for transfers between devices: 120 us -> 110 us  [local(): sum_second = lax.psum(own_second, ('row', 'col'))]
    all_to_all x0 -> x1, local copies, waits for them, and re-layouts: none -> 9.95 us  [local(): lax.all_to_all(jnp.stack([partials] * lax.axis_size('col')), 'col', 0, 0)]
  transfers between devices with their start and end apart: 4 -> 4, of which waited for: 4 -> 3; matrix products, arithmetic and copies ran while one was open for 24% -> 8% of each run, Pallas kernels for 0% -> 0%
where the time goes in v1:
time: 906 us; the launch traced here: 905 us
  blocking collectives  469 us (52%)
  waiting for transfers between devices  247 us (27%)
  other arithmetic  66.5 us (7%)
  matrix products  51 us (6%)
  local copies, waits for them, and re-layouts  46.8 us (5%)
  between operations  17.8 us (2%)
    unnamed x1, blocking collectives  469 us
    psum x1, waiting for transfers between devices, local(): sum_second = lax.psum(own_second, ('row', 'col'))  110 us
    psum x1, waiting for transfers between devices, local(): sum_third = lax.psum(own_third, 'col')  95.4 us
    all_gather x1, waiting for transfers between devices, local(): shard_piece = lax.all_gather(mode2_factor, 'row', axis=0, tiled=True)  40.6 us
    dot_general x6, matrix products, contract(): jnp.einsum('gie,ger->gir', values_part, khatri, precision=HIGHEST_PRECISION)  36.6 us
    another operation x6, other arithmetic, local(): cholesky_factor = jnp.linalg.cholesky(normal_matrix)  34 us
    another operation x3, other arithmetic, local(): return jax.scipy.linalg.cho_solve((cholesky_factor, True), mttkrp_rows.T).T  19.7 us
  transfers between devices with their start and end apart: 4, of which 3 were waited for; matrix products, arithmetic and copies ran while one was open for 8% of the time, Pallas kernels for 0%

profile of v1, /device:TPU:1, one launch (start us, length us, event | category | flops | bytes accessed | tf_op | source)
XLA Modules:
  0.0 905.0 jit_solution(6734943769744892875)
XLA Ops:
  10.5 3.7 gather_fusion.1
  15.8 40.6 %all-gather.2.cloned.1.call-done = f32[4096,256]{1,0:T(8,128)} async-done(((f32[256,256]{1,0:T(8,128)}), f32[4096,256]{1,0:T(8,128)}) %all-gather.2.cloned.1.call-update) | async-done | bytes 4194320 | tf_op jit(solution)/shard_map/all_gather | solution.py:48
  56.4 5.8 gather_fusion
  62.2 1.5 select_select_fusion
  63.9 53.0 %while.11 = (s32[]{:T(128)}, f32[48,32,256]{2,0,1:T(8,128)S(1)}, s32[]{:T(128)}, f32[48,32,1024]{2,1,0:T(8,128)}, f32[48,32,256]{2,1,0:T(8,128)}, /*index=5*/f32...) while((s32[]{:T(128)}, f32[48,32,256]{2,0,1:T(8,128)S(1)}, ...), condition=%wide.region_7.8_spmd, body=%wide.region_6.7_spmd.sunk | while | flops 807403520 | bytes 20709556 | solution.py:72
  66.2 6.1 fusion.52
  75.0 6.1 fusion.52
  83.8 6.1 fusion.52
  92.7 6.1 fusion.52
  101.5 6.1 fusion.52
  110.3 6.1 fusion.52
  116.9 11.6 %stack.2 = f32[16,48,32,256]{3,1,2,0:T(8,128)} broadcast(f32[48,32,256]{2,0,1:T(8,128)S(1)} %get-tuple-element.38), dimensions={1,2,3} | broadcast | bytes 26738688 | tf_op jit(solution)/shard_map/stack | solution.py:78
  128.5 6.7 all-to-all-start
  136.7 1.7 fusion.32
  139.9 468.7 %all-reduce.1 = f32[768]{0:T(1024)S(1)} all-reduce(f32[768]{0:T(1024)S(1)} %convert_dynamic-update-slice_fusion), channel_id=1, replica_groups=mesh['row'=16,'col'=16] {'col'}, use_global_device_ids=true, to_apply=%add.1 | all-reduce | flops 768 | bytes 6144
  608.7 110.2 %all-reduce.5.cloned.1.call-done = f32[256,256]{0,1:T(8,128)} async-done(((f32[256,256]{0,1:T(8,128)}), f32[256,256]{0,1:T(8,128)}) %all-reduce.5.cloned.1.call-update) | async-done | bytes 262160 | tf_op jit(solution)/shard_map/psum | solution.py:44
  718.8 95.4 %all-reduce.7.cloned.1.call-done = f32[256,256]{0,1:T(8,128)} async-done(((f32[256,256]{0,1:T(8,128)}), f32[256,256]{0,1:T(8,128)}) %all-reduce.7.cloned.1.call-update) | async-done | bytes 262160 | tf_op jit(solution)/shard_map/psum | solution.py:45
  815.4 11.7 %cholesky.50 = f32[128,128]{1,0:T(8,128)S(1)} custom-call(f32[128,128]{1,0:T(8,128)S(1)} %cholesky.118), custom_call_target="Cholesky" | custom-call | tf_op jit(solution)/shard_map/jit(cholesky)/cholesky | solution.py:83
  827.2 9.8 %custom-call.18 = f32[1,128,128]{1,2,0:T(8,128)S(1)} custom-call(f32[1,128,128]{2,1,0:T(8,128)S(1)} %get-tuple-element.74), custom_call_target="InvertDiagBlocksLowerTriangular" | custom-call | tf_op jit(solution)/shard_map/jit(cholesky)/cholesky | solution.py:83
  837.5 11.7 %cholesky.105 = f32[128,128]{1,0:T(8,128)S(1)} custom-call(f32[128,128]{1,0:T(8,128)S(1)} %convolution_subtract_fusion.2), custom_call_target="Cholesky" | custom-call | tf_op jit(solution)/shard_map/jit(cholesky)/cholesky | solution.py:83
  851.3 4.1 while.12
  855.4 19.7 %custom-call.19 = f32[2,128,128]{1,2,0:T(8,128)S(1)} custom-call(f32[2,128,128]{2,1,0:T(8,128)S(1)} %get-tuple-element.46), custom_call_target="InvertDiagBlocksLowerTriangular" | custom-call | tf_op jit(solution)/shard_map/jit(_cho_solve)/triangular_solve | solution.py:85
  875.1 9.9 %copy.25 = f32[16,48,32,256]{3,1,0,2:T(8,128)S(1)} copy(f32[16,48,32,256]{3,1,2,0:T(8,128)} %all-to-all-done) | data formatting | bytes 50331648 | tf_op jit(solution)/shard_map/all_to_all | solution.py:78
  885.0 8.5 fusion.14
  (90 shorter events, 32.8 us)
Async XLA Ops:
  7.4 3.1 copy-start
  7.4 49.0 %all-gather.2.cloned.1.call-start = ((), (), s32[]{:S(2)}) async-start(), calls=%async_computation.3 | async-start | bytes 4456448 | tf_op jit(solution)/shard_map/all_gather | solution.py:48
  128.5 6.8 copy-start.1
  128.5 746.6 %all-to-all-start = ((f32[16,48,32,256]{3,1,2,0:T(8,128)}), f32[16,48,32,256]{3,1,2,0:T(8,128)}, u32[]{:S(2)}, u32[]{:S(2)}) async-start(f32[16,48,32,256]{3,1,2,0:T(8,128)} %stack.2), calls=%async_computation | async-start | bytes 50331648 | tf_op jit(solution)/shard_map/all_to_all | solution.py:78
  135.2 3.2 copy-start.4
  135.2 4.6 copy-start.2
  135.3 4.6 copy-start.3
  135.3 583.6 %all-reduce.5.cloned.1.call-start = ((), (), s32[]{:S(2)}) async-start(), calls=%async_computation.1 | async-start | bytes 524288 | tf_op jit(solution)/shard_map/psum | solution.py:44
  136.7 677.5 %all-reduce.7.cloned.1.call-start = ((), (), s32[]{:S(2)}) async-start(), calls=%async_computation.2 | async-start | bytes 524288 | tf_op jit(solution)/shard_map/psum | solution.py:45
Sparse Core Ops, SparseCore 0:
  10.0 46.3 all-gather.1
Sparse Core Ops, SparseCore 1:
  141.2 577.6 all-reduce.4
  721.9 92.3 all-reduce.6
